TPU v7x, 128 devices: a whole 4x4x4 slice. The times are simulated.
128 devices in a mesh: col: 4 (over z), rhs: 32 (over x, y, core).
Axes of the slice: x: 4, y: 4, z: 4, core: 2. Of those that a mesh axis runs over, the one named last changes fastest.
Arguments:
- desc_rows: bfloat16 [128, 4096, 1024], P(('col', 'rhs')), may hold values from -6 to 6
- upd_factor: bfloat16 [128, 1024, 1024], P(('col', 'rhs')), may hold values from -0.03125 to 0.03125
- update_index: int32 [128, 1024], P(('col', 'rhs')), may hold values from -1 to 1023, as said below
- owner_map: int32 [128, 4], P(('col', 'rhs')), may hold values from 0 to 3, each once within a row
- sep_rhs: float32 [4096, 4096], P('rhs', 'col'), may hold values from -6 to 6
- factor_rows: bfloat16 [4096, 4096], P('col'), may hold values from -0.046875 to 0.046875
- diag_inverse: bfloat16 [4096, 1024], P('col'), may hold values from -1 to 1
Outputs:
- solved: float32 [4096, 4096], P('rhs', 'col')
Inputs may be any that keep to these rules, and one draw needn't show every extreme that they name: `update_index`: within each group of 256 slots of a descendant the live entries come first and are distinct rows of the block that owner_map names for that group; the other slots hold -1. Every descendant has at least one group with all 256 slots live.
All inputs are finite; a program needn't handle non-finite values.
Results may differ from a plain program's by a relative error of at most 0.004.
Values sent between devices are 32-bit elements; how exact they have to be, the bound alone decides.
A program may use at most 128 MiB of HBM per device.

v0:
```python
import jax
import jax.numpy as jnp
from jax import lax
from jax.sharding import PartitionSpec as P


def passed_along(value, axis, steps):
    count = lax.axis_size(axis)
    first, last = (max(0, -steps), min(count, count - steps))
    return lax.ppermute(value, axis, [(source, source + steps) for source in range(first, last)])


def block_order(owner_row, count):
    places = jnp.arange(count, dtype=jnp.int32)
    matches = (owner_row[None, :] == places[:, None]).astype(jnp.int32)
    return jnp.sum(matches * places[None, :], axis=1)


def local(desc_rows, upd_factor, update_index, owner_map, sep_rhs, factor_rows, diag_inverse):
    col_count = lax.axis_size("col")
    rhs_count = lax.axis_size("rhs")
    block_size = diag_inverse.shape[0]
    tile_rows = sep_rhs.shape[0]
    full_width = factor_rows.shape[1]
    capacity = update_index.shape[1] // col_count
    source_group = block_order(owner_map[0], col_count)
    factor_grouped = jnp.take(
        upd_factor[0].reshape(block_size, col_count, capacity), source_group, axis=1
    )
    local_index = jnp.take(update_index[0].reshape(col_count, capacity), source_group, axis=0)
    updates = jnp.einsum(
        "srn,ngc->gscr",
        desc_rows[0].reshape(rhs_count, tile_rows, block_size),
        factor_grouped,
        preferred_element_type=jnp.float32,
    )
    index_copies = jnp.broadcast_to(local_index[:, None, :], (col_count, rhs_count, capacity))
    arrived, arrived_index = (
        lax.all_to_all(
            updates.reshape(col_count * rhs_count, capacity, tile_rows),
            ("col", "rhs"),
            split_axis=0,
            concat_axis=0,
            tiled=True,
        ),
        lax.all_to_all(
            index_copies.reshape(col_count * rhs_count, capacity),
            ("col", "rhs"),
            split_axis=0,
            concat_axis=0,
            tiled=True,
        ),
    )
    targets = jnp.where(arrived_index >= 0, arrived_index, block_size).reshape(-1)
    summed = jax.ops.segment_sum(
        arrived.reshape(-1, tile_rows), targets, num_segments=block_size + 1
    )
    corrected = sep_rhs - summed[:block_size].T
    own_place = lax.axis_index("col")
    result = jnp.zeros((tile_rows, block_size), jnp.float32)
    carried = jnp.zeros((tile_rows, full_width), jnp.float32)
    for station in range(col_count):
        begin = station * block_size

        def advance_rest(carry_state, begin=begin):
            pending = carry_state[1]
            reduced = corrected - pending[:, :block_size]
            solved = jnp.dot(
                reduced.astype(jnp.bfloat16), diag_inverse, preferred_element_type=jnp.float32
            )
            pending = pending + jnp.dot(
                solved.astype(jnp.bfloat16),
                factor_rows[:, begin:],
                preferred_element_type=jnp.float32,
            )
            return (solved, pending)

        result, carried = lax.cond(
            own_place == station, advance_rest, lambda carry_state: carry_state, (result, carried)
        )
        if station + 1 < col_count:
            carried = passed_along(carried[:, block_size:], "col", 1)
    return result


def solution(mesh):
    placed = (
        P(("col", "rhs"), None, None),
        P(("col", "rhs"), None, None),
        P(("col", "rhs"), None),
        P(("col", "rhs"), None),
        P("rhs", "col"),
        P("col", None),
        P("col", None),
    )
    return jax.shard_map(
        local, mesh=mesh, in_specs=placed, out_specs=P("rhs", "col"), check_vma=False
    )
```

profile of v0, /device:TPU:96, one launch (start us, length us, event | category | flops | bytes accessed | tf_op | source)
XLA Modules:
  0.0 563.5 jit_solution(13394403649283383194)
XLA Ops:
  1.3 1.3 reduce.3
  4.1 9.9 %all-to-all-start = ((s32[128,1,256]{2,1,0:T(1,128)}), s32[128,1,256]{2,1,0:T(1,128)S(1)}, u32[]{:S(2)}, u32[]{:S(2)}) async-start(s32[128,1,256]{2,1,0:T(1,128)} %all_to_all.11), calls=%async_computation | async-start | bytes 262144 | tf_op jit(solution)/shard_map/all_to_all | solution.py:46
  14.0 3.9 copy.33
  17.9 2.8 copy.34
  20.8 2.0 gather_fusion.1
  22.8 15.0 %fusion.19 = f32[4,256,32,128]{3,1,2,0:T(8,128)} fusion(bf16[32,128,1024,1]{2,1,0,3:T(8,128)(2,1)} %bitcast.37, bf16[4,1024,256]{2,1,0:T(8,128)(2,1)} %gather_fusion.1, pred[4]{0:T(512)(128)(4,1)S(1)} %compare_and_fusion), kind=kOutput, calls=%fused_computation.21 | convolution fusion | flops 8590983168 | bytes 27262980 | tf_op jit(solution)/shard_map/srn,ngc->gscr/dot_general | solution.py:31
  37.8 10.2 %all-to-all-start.1 = ((f32[128,256,128]{2,1,0:T(8,128)}), f32[128,256,128]{2,1,0:T(8,128)}, u32[]{:S(2)}, u32[]{:S(2)}) async-start(f32[128,256,128]{2,1,0:T(8,128)} %bitcast.33), calls=%async_computation.1 | async-start | bytes 33554432 | tf_op jit(solution)/shard_map/all_to_all | solution.py:39
  48.0 1.0 copy.36
  49.2 210.7 %all-to-all-done.1 = f32[128,256,128]{2,1,0:T(8,128)} async-done(((f32[128,256,128]{2,1,0:T(8,128)}), f32[128,256,128]{2,1,0:T(8,128)}, u32[]{:S(2)}, u32[]{:S(2)}) %all-to-all-start.1) | async-done | bytes 16777248 | tf_op jit(solution)/shard_map/all_to_all | solution.py:39
  259.9 191.7 %scatter_custom_fusion = f32[1025,128]{1,0:T(8,128)S(1)} fusion(s32[32768]{0:T(1024)S(1)} %bitcast.36, f32[32768,128]{1,0:T(8,128)} %bitcast.12, f32[]{:T(128)} %constant.34.clone.1), kind=kCustom, calls=%fused_computation.29 | custom fusion | flops 4194304 | bytes 525312 | tf_op jit(solution)/shard_map/scatter-add | solution.py:55
  451.7 1.1 fusion.24
  452.8 2.4 conditional.4
  452.8 1.6 broadcast_in_dim.33
  455.2 2.7 slice.25
  457.9 1.3 collective-permute-start
  459.2 39.7 %collective-permute-done = f32[128,3072]{1,0:T(8,128)} collective-permute-done((f32[128,3072]{1,0:T(8,128)}, f32[128,3072]{1,0:T(8,128)}, u32[]{:S(2)}, u32[]{:S(2)}) %collective-permute-start) | collective-permute-done | bytes 1572896 | tf_op jit(solution)/shard_map/ppermute | solution.py:10
  498.9 2.3 slice.26
  501.2 1.3 collective-permute-start.1
  502.5 24.4 %collective-permute-done.1 = f32[128,2048]{1,0:T(8,128)} collective-permute-done((f32[128,2048]{1,0:T(8,128)}, f32[128,2048]{1,0:T(8,128)}, u32[]{:S(2)}, u32[]{:S(2)}) %collective-permute-start.1) | collective-permute-done | bytes 1048608 | tf_op jit(solution)/shard_map/ppermute | solution.py:10
  526.9 1.9 slice.27
  528.8 1.3 collective-permute-start.2
  530.1 30.1 %collective-permute-done.2 = f32[128,1024]{1,0:T(8,128)S(1)} collective-permute-done((f32[128,1024]{1,0:T(8,128)}, f32[128,1024]{1,0:T(8,128)S(1)}, u32[]{:S(2)}, u32[]{:S(2)}) %collective-permute-start.2) | collective-permute-done | bytes 524320 | tf_op jit(solution)/shard_map/ppermute | solution.py:10
  560.2 3.3 conditional.7
  561.2 2.3 fusion.18
  (22 shorter events, 4.7 us)
Async XLA Ops:
  4.1 33.7 %all-to-all-start = ((s32[128,1,256]{2,1,0:T(1,128)}), s32[128,1,256]{2,1,0:T(1,128)S(1)}, u32[]{:S(2)}, u32[]{:S(2)}) async-start(s32[128,1,256]{2,1,0:T(1,128)} %all_to_all.11), calls=%async_computation | async-start | bytes 262144 | tf_op jit(solution)/shard_map/all_to_all | solution.py:46
  37.8 10.2 %copy-start.2 = (f32[128,1024]{1,0:T(8,128)S(1)}, f32[128,1024]{1,0:T(8,128)}, u32[]{:S(2)}) copy-start(f32[128,1024]{1,0:T(8,128)} %param.19) | copy-start | bytes 1572868
  37.8 222.1 %all-to-all-start.1 = ((f32[128,256,128]{2,1,0:T(8,128)}), f32[128,256,128]{2,1,0:T(8,128)}, u32[]{:S(2)}, u32[]{:S(2)}) async-start(f32[128,256,128]{2,1,0:T(8,128)} %bitcast.33), calls=%async_computation.1 | async-start | bytes 33554432 | tf_op jit(solution)/shard_map/all_to_all | solution.py:39
  48.0 404.7 %copy-start = (bf16[1024,1024]{1,0:T(8,128)(2,1)S(1)}, bf16[1024,1024]{1,0:T(8,128)(2,1)}, u32[]{:S(2)}) copy-start(bf16[1024,1024]{1,0:T(8,128)(2,1)} %param.21) | copy-start | bytes 6291460
  457.9 41.0 %collective-permute-start = (f32[128,3072]{1,0:T(8,128)}, f32[128,3072]{1,0:T(8,128)}, u32[]{:S(2)}, u32[]{:S(2)}) collective-permute-start(f32[128,3072]{1,0:T(8,128)} %slice.25), channel_id=1, source_target_pairs={{0,32},{32,64},{64,96},{1,33},{33,65},{65,97},{2,34},{34,66},{66,9... | collective-permute-start | bytes 4718600 | tf_op jit(solution)/shard_map/ppermute | solution.py:10
  501.2 25.7 %collective-permute-start.1 = (f32[128,2048]{1,0:T(8,128)}, f32[128,2048]{1,0:T(8,128)}, u32[]{:S(2)}, u32[]{:S(2)}) collective-permute-start(f32[128,2048]{1,0:T(8,128)} %slice.26), channel_id=1, source_target_pairs={{0,32},{32,64},{64,96},{1,33},{33,65},{65,97},{2,34},{34,66},{66,9... | collective-permute-start | bytes 3145736 | tf_op jit(solution)/shard_map/ppermute | solution.py:10
  528.8 31.4 %collective-permute-start.2 = (f32[128,1024]{1,0:T(8,128)}, f32[128,1024]{1,0:T(8,128)S(1)}, u32[]{:S(2)}, u32[]{:S(2)}) collective-permute-start(f32[128,1024]{1,0:T(8,128)} %slice.27), channel_id=1, source_target_pairs={{0,32},{32,64},{64,96},{1,33},{33,65},{65,97},{2,34},{34,66},{66,9... | collective-permute-start | bytes 1572872 | tf_op jit(solution)/shard_map/ppermute | solution.py:10
  560.2 0.8 copy-start.1
where the time goes:
time: 570 us; the launch traced here: 563 us
  waiting for transfers between devices  305 us (54%)
  other arithmetic  195 us (34%)
  starting transfers between devices  23.9 us (4%)
  local copies, waits for them, and re-layouts  22 us (4%)
  matrix products  17.3 us (3%)
    all_to_all x1, waiting for transfers between devices, local(): lax.all_to_all(updates.reshape(col_count * rhs_count, capacity, tile_rows...  211 us
    scatter-add x1, other arithmetic, local(): jax.ops.segment_sum(arrived.reshape(-1, tile_rows), targets, num_segments...  192 us
    ppermute x3, waiting for transfers between devices, passed_along(): lax.ppermute(value, axis, [(source, source + steps) for source in range(f...  94.2 us
    dot_general x1, matrix products, local(): jnp.einsum('srn,ngc->gscr', desc_rows[0].reshape(rhs_count, tile_rows, bl...  15 us
  transfers between devices with their start and end apart: 5, of which 4 were waited for; matrix products, arithmetic and copies ran while one was open for 4% of the time, Pallas kernels for 0%

commit v1 on v0

v1 whole, which is shorter than its diff:
```python
import functools

import jax
import jax.numpy as jnp
from jax import lax
from jax.experimental import pallas as pl
from jax.experimental.pallas import tpu as pltpu
from jax.sharding import PartitionSpec as P

MESH = pl.DeviceIdType.MESH
CHUNKS = 4
ORDERS = ((0, 2, 1), (2, 1, 0), (1, 0, 2), (0, 2, 1))


def flip(place, bit):
    low = place + 1 - 2 * lax.rem(place, 2)
    high = 3 - place
    return (1 - bit) * low + bit * high


def flip_if(place, bit, wanted):
    return place + wanted * (flip(place, bit) - place)


def kernel(owner, index, desc, factor, sep, rows_factor, inverse, out,
           left, fac_raw, fac, send, recv, index_send, index_recv, columns, onehot, wide,
           dense, half0, half1, half2, half3, base, corrected, pend_out, pend_in,
           load_sem, misc_sem, late_sem, index_ssem, index_rsem, s1_ssem, s1_rsem,
           h_ssem, h_rsem, p_ssem, p_rsem):
    block = inverse.shape[0]
    cap = index.shape[1] // 4
    tile = sep.shape[0]
    size = tile // CHUNKS
    halves = (half0, half1, half2, half3)

    z = lax.axis_index("col")
    rhs = lax.axis_index("rhs")
    core = lax.rem(rhs, 2)
    y = lax.rem(lax.div(rhs, 2), 4)
    x = lax.div(rhs, 8)
    star, rest = core, 1 - core

    def device(zz, yy, xx, kk):
        return (zz, (xx * 4 + yy) * 2 + kk)

    def other(kappa):
        return core + kappa * (1 - 2 * core)

    def star_peer(kappa, n):
        kk = other(kappa)
        return device(
            flip(z, kk) if n == 3 else z,
            flip(y, kk) if n == 2 else y,
            flip(x, kk) if n == 1 else x,
            kk,
        )

    def rest_peer(axis):
        return device(
            flip(z, rest) if axis == 0 else z,
            flip(y, rest) if axis == 1 else y,
            flip(x, rest) if axis == 2 else x,
            core,
        )

    antipode = device(flip(z, star), flip(y, star), flip(x, star), core)

    barrier = pltpu.get_barrier_semaphore()
    greeted = [device(z, y, x, 1 - core), antipode]
    for kk in (core, 1 - core):
        for bit in (0, 1):
            greeted.append(device(flip(z, bit), y, x, kk))
            greeted.append(device(z, flip(y, bit), x, kk))
            greeted.append(device(z, y, flip(x, bit), kk))
    greeted.append(device(lax.rem(z + 2, 4), y, x, core))
    for peer in greeted:
        pl.semaphore_signal(barrier, inc=1, device_id=peer, device_id_type=MESH)

    fac_copy = pltpu.make_async_copy(factor.at[0], fac_raw, misc_sem.at[0])
    fac_copy.start()
    for t in range(CHUNKS):
        def load(i, carry, t=t):
            kk = other(lax.div(i, 16))
            jx, jy = lax.rem(lax.div(i, 8), 2), lax.rem(lax.div(i, 4), 2)
            ry, rx = lax.rem(lax.div(i, 2), 2), lax.rem(i, 2)
            xx = flip_if(flip_if(x, kk, jx), 1 - kk, rx)
            yy = flip_if(flip_if(y, kk, jy), 1 - kk, ry)
            begin = ((xx * 4 + yy) * 2 + kk) * tile + t * size
            pltpu.make_async_copy(
                desc.at[0, pl.ds(pl.multiple_of(begin, size), size), :],
                left.at[t, pl.ds(pl.multiple_of(i * size, size), size), :],
                load_sem.at[t],
            ).start()
            return carry
        lax.fori_loop(0, 32, load, 0)
    base_copy = pltpu.make_async_copy(sep, base, misc_sem.at[1])
    base_copy.start()

    index_send[...] = jnp.full(index_send.shape, -1, jnp.int32)
    for blk in range(4):
        total = jnp.zeros((1, cap), jnp.int32)
        for g in range(4):
            total = total + index[0:1, g * cap : (g + 1) * cap] * (owner[0, g] == blk).astype(jnp.int32)
        index_send[blk : blk + 1, :] = total
    fac_copy.wait()

    def order_factor(i, carry):
        rows = pl.ds(pl.multiple_of(i * 128, 128), 128)
        for blk in range(4):
            total = fac_raw[rows, :cap]
            for g in range(1, 4):
                total = jnp.where(owner[0, g] == blk, fac_raw[rows, g * cap : (g + 1) * cap], total)
            fac[blk, rows, :] = total
        return carry

    lax.fori_loop(0, block // 128, order_factor, 0)

    def updates(t):
        slot = t % 2
        pltpu.make_async_copy(left.at[t], left.at[t], load_sem.at[t]).wait()

        def step(i, carry):
            kappa = 1 - lax.div(i, 4)
            dz0, dz1 = lax.rem(lax.div(i, 2), 2), lax.rem(i, 2)
            kk = other(kappa)
            zz = flip_if(flip_if(z, kk, dz0), 1 - kk, dz1)
            weights = fac[zz]
            for j, (n, a) in enumerate(((3 * dz0, 0), (2 - dz0, dz0), (1 + dz0, dz0), (3 - 3 * dz0, 1))):
                begin = (kappa * 16 + j * 4) * size
                rows = left[t, pl.ds(pl.multiple_of(begin, size), 4 * size), :]
                send[slot, kappa, n, a, dz1] = jnp.dot(
                    rows, weights, preferred_element_type=jnp.float32
                )
            return carry

        lax.fori_loop(0, 8, step, 0)

    def stage1(t, kappa, n):
        return pltpu.make_async_remote_copy(
            src_ref=send.at[t % 2, kappa, n],
            dst_ref=recv.at[t, kappa * 4 + n - 1],
            send_sem=s1_ssem.at[t % 2, kappa * 4 + n - 1],
            recv_sem=s1_rsem.at[t, kappa * 4 + n - 1],
            device_id=star_peer(kappa, n),
            device_id_type=MESH,
        )

    messages = [(1, 3), (1, 2), (1, 1), (0, 3), (0, 2), (0, 1), (1, 0)]

    def start_stage1(t):
        for kappa, n in messages:
            stage1(t, kappa, n).start()

    def index_copy(kappa, n):
        return pltpu.make_async_remote_copy(
            src_ref=index_send,
            dst_ref=index_recv.at[kappa * 4 + n],
            send_sem=index_ssem.at[kappa * 4 + n - 1],
            recv_sem=index_rsem.at[kappa * 4 + n - 1],
            device_id=star_peer(kappa, n),
            device_id_type=MESH,
        )

    def own_block(a, rz):
        return flip_if(flip_if(z, star, a), rest, rz)

    def index_columns():
        for kappa, n in messages:
            index_copy(kappa, n).wait()
        index_recv[0] = index_send[...]

        def step(i, carry):
            zz = own_block(lax.div(i, 2), lax.rem(i, 2))
            rows = [index_recv[m, pl.ds(zz, 1), :] for m in range(8)]
            rows = jnp.concatenate(rows + [jnp.full((120, cap), -1, jnp.int32)], axis=0)
            columns[i] = rows.T
            return carry

        lax.fori_loop(0, 4, step, 0)

    def assemble(t):
        for kappa, n in messages:
            stage1(t, kappa, n).wait_recv()

        def step(i, carry):
            a, rz = lax.div(i, 2), lax.rem(i, 2)
            listed = columns[i]
            lanes = lax.broadcasted_iota(jnp.int32, (cap, block), 1)
            for m in range(8):
                piece = send[t % 2, 0, 0, a, rz] if m == 0 else recv[t, m - 1, a, rz]
                wide[:, m * cap : (m + 1) * cap] = piece.astype(jnp.bfloat16)
                chosen = listed[:, m : m + 1] == lanes
                onehot[m * cap : (m + 1) * cap, :] = jnp.where(chosen, 1.0, 0.0).astype(jnp.bfloat16)
            total = jnp.dot(wide[...], onehot[...], preferred_element_type=jnp.float32)
            dense[t, a, rz] = total.reshape(2, 2, size, block)
            return carry

        lax.fori_loop(0, 4, step, 0)

    def part(t, stage, side):
        if stage == 3:
            return (t, side, 0, 0, 0)
        where = [slice(None)] * 3
        for axis in ORDERS[t][:stage]:
            where[axis] = 0
        where[ORDERS[t][stage]] = side
        return (t, slice(None), *where)

    def halving(t, stage):
        return pltpu.make_async_remote_copy(
            src_ref=dense.at[part(t, stage, 1)],
            dst_ref=halves[stage].at[t],
            send_sem=h_ssem.at[t, stage],
            recv_sem=h_rsem.at[t, stage],
            device_id=antipode if stage == 3 else rest_peer(ORDERS[t][stage]),
            device_id_type=MESH,
        )

    def add_half(t, stage):
        halving(t, stage).wait_recv()
        where = part(t, stage, 0)
        dense[where] = dense[where] + halves[stage][t]

    def first(t):
        assemble(t)
        halving(t, 0).start()

    def later(t, stage):
        add_half(t, stage - 1)
        halving(t, stage).start()

    def last(t):
        halving(t, 3).wait_recv()
        rows = slice(t * size, (t + 1) * size)
        corrected[rows, :] = base[rows, :] - (dense[t, 0, 0, 0, 0] + half3[t])

    def late_load(d):
        begin = pl.multiple_of((z + d) * block, block)
        return pltpu.make_async_copy(
            rows_factor.at[:, pl.ds(begin, block)], left.at[d - 1], late_sem.at[d]
        )

    inverse_load = pltpu.make_async_copy(inverse, left.at[3], late_sem.at[0])

    updates(0)
    pl.semaphore_wait(barrier, len(greeted))
    for kappa, n in messages:
        index_copy(kappa, n).start()
    start_stage1(0)
    updates(1)
    start_stage1(1)
    index_columns()
    first(0)
    for kappa, n in messages:
        stage1(0, kappa, n).wait_send()
    updates(2)
    start_stage1(2)
    first(1)
    later(0, 1)
    for kappa, n in messages:
        stage1(1, kappa, n).wait_send()
    updates(3)
    start_stage1(3)
    for d in range(1, 4):
        @pl.when(z + d < 4)
        def _(d=d):
            late_load(d).start()
    inverse_load.start()
    first(2)
    later(1, 1)
    later(0, 2)
    first(3)
    base_copy.wait()
    later(2, 1)
    later(1, 2)
    later(0, 3)
    later(3, 1)
    later(2, 2)
    later(1, 3)
    last(0)
    later(3, 2)
    later(2, 3)
    last(1)
    later(3, 3)
    last(2)
    last(3)
    for d in range(1, 4):
        @pl.when(z + d < 4)
        def _(d=d):
            late_load(d).wait()
    inverse_load.wait()

    def pending(station, d, t):
        rows = pl.ds(t * size, size)
        return pltpu.make_async_remote_copy(
            src_ref=pend_out.at[d - 1, rows, :],
            dst_ref=pend_in.at[station, rows, :],
            send_sem=p_ssem.at[d - 1, t],
            recv_sem=p_rsem.at[station, t],
            device_id=device(station + d, y, x, core),
            device_id_type=MESH,
        )

    for station in range(4):
        @pl.when(z == station)
        def _(station=station):
            for t in range(CHUNKS):
                rows = slice(t * size, (t + 1) * size)
                reduced = corrected[rows, :]
                for earlier in range(station):
                    pending(earlier, station - earlier, t).wait_recv()
                    reduced = reduced - pend_in[earlier, rows, :]
                solved = jnp.dot(
                    reduced.astype(jnp.bfloat16), left[3], preferred_element_type=jnp.float32
                )
                out[rows, :] = solved
                for d in range(1, 4 - station):
                    pend_out[d - 1, rows, :] = jnp.dot(
                        solved.astype(jnp.bfloat16), left[d - 1], preferred_element_type=jnp.float32
                    )
                    pending(station, d, t).start()
            for t in range(CHUNKS):
                for d in range(1, 4 - station):
                    pending(station, d, t).wait_send()

    for kappa, n in messages:
        stage1(2, kappa, n).wait_send()
        stage1(3, kappa, n).wait_send()
    for t in range(CHUNKS):
        for stage in range(4):
            halving(t, stage).wait_send()


def local(desc_rows, upd_factor, update_index, owner_map, sep_rhs, factor_rows, diag_inverse):
    tile, block = sep_rhs.shape
    cap = update_index.shape[1] // 4
    size = tile // CHUNKS
    f32, bf16, i32 = jnp.float32, jnp.bfloat16, jnp.int32
    vmem = pl.BlockSpec(memory_space=pltpu.VMEM)
    hbm = pl.BlockSpec(memory_space=pl.ANY)
    dma = pltpu.SemaphoreType.DMA
    return pl.pallas_call(
        kernel,
        out_shape=jax.ShapeDtypeStruct((tile, block), f32),
        in_specs=[pl.BlockSpec(memory_space=pltpu.SMEM), vmem, hbm, hbm, hbm, hbm, hbm],
        out_specs=vmem,
        scratch_shapes=[
            pltpu.VMEM((CHUNKS, 32 * size, block), bf16),
            pltpu.VMEM((block, 4 * cap), bf16),
            pltpu.VMEM((4, block, cap), bf16),
            pltpu.VMEM((2, 2, 4, 2, 2, 4 * size, cap), f32),
            pltpu.VMEM((CHUNKS, 7, 2, 2, 4 * size, cap), f32),
            pltpu.VMEM((8, cap), i32),
            pltpu.VMEM((8, 8, cap), i32),
            pltpu.VMEM((4, cap, 128), i32),
            pltpu.VMEM((8 * cap, block), bf16),
            pltpu.VMEM((4 * size, 8 * cap), bf16),
            pltpu.VMEM((CHUNKS, 2, 2, 2, 2, size, block), f32),
            pltpu.VMEM((CHUNKS, 2, 2, 2, size, block), f32),
            pltpu.VMEM((CHUNKS, 2, 2, size, block), f32),
            pltpu.VMEM((CHUNKS, 2, size, block), f32),
            pltpu.VMEM((CHUNKS, size, block), f32),
            pltpu.VMEM((tile, block), f32),
            pltpu.VMEM((tile, block), f32),
            pltpu.VMEM((3, tile, block), f32),
            pltpu.VMEM((3, tile, block), f32),
            dma((CHUNKS,)),
            dma((2,)),
            dma((4,)),
            dma((7,)),
            dma((7,)),
            dma((2, 7)),
            dma((CHUNKS, 7)),
            dma((CHUNKS, 4)),
            dma((CHUNKS, 4)),
            dma((3, CHUNKS)),
            dma((3, CHUNKS)),
        ],
        compiler_params=pltpu.CompilerParams(
            collective_id=0, has_side_effects=True, vmem_limit_bytes=67_000_000
        ),
    )(owner_map, update_index, desc_rows, upd_factor, sep_rhs, factor_rows, diag_inverse)


def solution(mesh):
    placed = (
        P(("col", "rhs"), None, None),
        P(("col", "rhs"), None, None),
        P(("col", "rhs"), None),
        P(("col", "rhs"), None),
        P("rhs", "col"),
        P("col", None),
        P("col", None),
    )
    return jax.shard_map(
        local, mesh=mesh, in_specs=placed, out_specs=P("rhs", "col"), check_vma=False
    )
```

time: 570 us -> 157 us (0.28); the launches traced: 563 us -> 157 us
  waiting for transfers between devices: 305 us -> 0 us
  other arithmetic: 195 us -> 0 us
  Pallas kernels: 0 us -> 155 us
  starting transfers between devices: 23.9 us -> 0 us
  local copies, waits for them, and re-layouts: 22 us -> 1.89 us
  matrix products: 17.3 us -> 0 us
    all_to_all x2 -> x0, waiting for transfers between devices: 211 us -> none  [the longest x1 211 us: local(): lax.all_to_all(updates.reshape(col_count * rhs_count, capacity, tile_rows...]
    scatter-add x1 -> x0, other arithmetic: 192 us -> none  [local(): jax.ops.segment_sum(arrived.reshape(-1, tile_rows), targets, num_segments...]
    pallas_call x0 -> x1, Pallas kernels: none -> 155 us  [local(): pl.pallas_call(kernel, out_shape=jax.ShapeDtypeStruct((tile, block), f32)...]
    ppermute x3 -> x0, waiting for transfers between devices: 94.2 us -> none  [passed_along(): lax.ppermute(value, axis, [(source, source + steps) for source in range(f...]
    all_to_all x2 -> x0, starting transfers between devices: 20.1 us -> none  [the longest x1 10.2 us: local(): lax.all_to_all(updates.reshape(col_count * rhs_count, capacity, tile_rows...]
    dot_general x2 -> x0, matrix products: 17.3 us -> none  [the longest x1 15 us: local(): jnp.einsum('srn,ngc->gscr', desc_rows[0].reshape(rhs_count, tile_rows, bl...]
    slice x3 -> x0, local copies, waits for them, and re-layouts: 6.93 us -> none  [local(): carried = passed_along(carried[:, block_size:], 'col', 1)]
  transfers between devices with their start and end apart: 5 -> 0, of which waited for: 4 -> 0; matrix products, arithmetic and copies ran while one was open for 4% -> 0% of each run, Pallas kernels for 0% -> 0%
where the time goes in v1:
time: 157 us
  Pallas kernels  155 us (99%)
  local copies, waits for them, and re-layouts  1.89 us (1%)
    pallas_call x1, Pallas kernels, local(): pl.pallas_call(kernel, out_shape=jax.ShapeDtypeStruct((tile, block), f32)...  155 us

profile of v1, /device:TPU:96, one launch (start us, length us, event | category | flops | bytes accessed | tf_op | source)
XLA Modules:
  0.0 156.6 jit_solution(17150089553765840740)
XLA Ops:
  0.0 154.7 %shard_map.73 = f32[128,1024]{1,0:T(8,128)} custom-call(s32[1,4]{1,0:T(1,128)} %owner.1, s32[1,1024]{1,0:T(1,128)} %index.1, bf16[1,4096,1024]{2,1,0:T(8,128)(2,1)} %desc.1, bf16[1,1024,1024]{2,1,0:T(8,128)(2,1)} %factor.1, f32[128,1024]{1,0:T(8,128)} %sep.1, bf16[1024,4096]{1,0:T(8,128)(2,1)} %rows_factor.1, bf16[1024,1024]{1,0:T(8,128)(2,1)} %inverse.1), custom_call_target="tpu_custom_call" | custom-call | tf_op jit(solution)/shard_map/pallas_call | solution.py:342
  154.7 1.9 %copy.9 = f32[128,1024]{1,0:T(8,128)} copy(f32[128,1024]{1,0:T(8,128)} %shard_map.73) | data formatting | bytes 1048576

commit v2 on v1

v2 whole, which is shorter than its diff:
```python
import functools

import jax
import jax.numpy as jnp
from jax import lax
from jax.experimental import pallas as pl
from jax.experimental.pallas import tpu as pltpu
from jax.sharding import PartitionSpec as P

MESH = pl.DeviceIdType.MESH
SIZES = (16, 32, 32, 32, 16)
STARTS = tuple(sum(SIZES[:t]) for t in range(len(SIZES)))
CHUNKS = len(SIZES)
SLOTS = 3
STRIPES = ((0, 384), (384, 384), (768, 256))
STEPS = (
    (0, 0), (0, 1), (1, 0), (0, 2), (1, 1), (0, 3), (2, 0), (1, 2),
    (0, 4), (2, 1), (1, 3), (3, 0), (2, 2), (1, 4), (3, 1), (2, 3),
    (4, 0), (3, 2), (2, 4), (5, 0), (4, 1), (3, 3), (4, 2), (3, 4),
    (4, 3), (5, 1), (4, 4), (5, 2), (5, 3), (5, 4),
)
LAGS = (0, 1, 2, 3)


def flip(place, bit):
    low = place + 1 - 2 * lax.rem(place, 2)
    high = 3 - place
    return (1 - bit) * low + bit * high


def flip_if(place, bit, wanted):
    return place + wanted * (flip(place, bit) - place)


def kernel(owner, index, desc, factor, sep, rows_factor, inverse, out,
           left, fac, own, index_send, index_recv, columns, onehot, wide, corrected, pend_in,
           load_sem, misc_sem, late_sem, index_ssem, index_rsem, s1_ssem, s1_rsem,
           h_ssem, h_rsem, a_ssem, a_rsem, p_ssem, p_rsem, *chunked):
    block = inverse.shape[0]
    cap = index.shape[1] // 4
    tile = sep.shape[0]
    send = chunked[:SLOTS]
    recv, dense, half0, half1, half2, half3 = (
        chunked[SLOTS + i * CHUNKS : SLOTS + (i + 1) * CHUNKS] for i in range(6)
    )
    halves = (half0, half1, half2)
    fac_raw = onehot.at[0:block]

    z = lax.axis_index("col")
    rhs = lax.axis_index("rhs")
    core = lax.rem(rhs, 2)
    y = lax.rem(lax.div(rhs, 2), 4)
    x = lax.div(rhs, 8)
    star, rest = core, 1 - core

    def device(zz, yy, xx, kk):
        return (zz, (xx * 4 + yy) * 2 + kk)

    def other(kappa):
        return core + kappa * (1 - 2 * core)

    def star_peer(kappa, n):
        kk = other(kappa)
        return device(
            flip(z, kk) if n == 3 else z,
            flip(y, kk) if n == 2 else y,
            flip(x, kk) if n == 1 else x,
            kk,
        )

    def rest_peer(axis):
        return device(
            flip(z, rest) if axis == 0 else z,
            flip(y, rest) if axis == 1 else y,
            flip(x, rest) if axis == 2 else x,
            core,
        )

    antipode = device(flip(z, star), flip(y, star), flip(x, star), core)

    barrier = pltpu.get_barrier_semaphore()
    greeted = [device(z, y, x, 1 - core), antipode]
    for kk in (core, 1 - core):
        for bit in (0, 1):
            greeted.append(device(flip(z, bit), y, x, kk))
            greeted.append(device(z, flip(y, bit), x, kk))
            greeted.append(device(z, y, flip(x, bit), kk))
    greeted.append(device(lax.rem(z + 2, 4), y, x, core))
    for peer in greeted:
        pl.semaphore_signal(barrier, inc=1, device_id=peer, device_id_type=MESH)

    fac_copy = pltpu.make_async_copy(factor.at[0], fac_raw, misc_sem.at[0])
    fac_copy.start()
    def load_rows(t):
        size = SIZES[t]

        def load(i, carry):
            kk = other(lax.div(i, 16))
            jx, jy = lax.rem(lax.div(i, 8), 2), lax.rem(lax.div(i, 4), 2)
            ry, rx = lax.rem(lax.div(i, 2), 2), lax.rem(i, 2)
            xx = flip_if(flip_if(x, kk, jx), 1 - kk, rx)
            yy = flip_if(flip_if(y, kk, jy), 1 - kk, ry)
            begin = ((xx * 4 + yy) * 2 + kk) * tile + STARTS[t]
            pltpu.make_async_copy(
                desc.at[0, pl.ds(pl.multiple_of(begin, 16), size), :],
                left.at[pl.ds(pl.multiple_of(32 * STARTS[t] + i * size, 16), size), :],
                load_sem.at[t],
            ).start()
            return carry

        lax.fori_loop(0, 32, load, 0)

    load_rows(0)
    base_copy = pltpu.make_async_copy(sep, corrected, misc_sem.at[1])

    index_send[...] = jnp.full(index_send.shape, -1, jnp.int32)
    for blk in range(4):
        total = jnp.zeros((1, cap), jnp.int32)
        for g in range(4):
            total = total + index[0:1, g * cap : (g + 1) * cap] * (owner[0, g] == blk).astype(jnp.int32)
        index_send[blk : blk + 1, :] = total
    fac_copy.wait()

    def order_factor(i, carry):
        rows = pl.ds(pl.multiple_of(i * 128, 128), 128)
        for blk in range(4):
            total = fac_raw[rows, :cap]
            for g in range(1, 4):
                total = jnp.where(owner[0, g] == blk, fac_raw[rows, g * cap : (g + 1) * cap], total)
            fac[blk, rows, :] = total
        return carry

    lax.fori_loop(0, block // 128, order_factor, 0)

    def updates(t):
        size, slot = SIZES[t], send[t % SLOTS]
        loaded = left.at[32 * STARTS[t] : 32 * (STARTS[t] + size)]
        pltpu.make_async_copy(loaded, loaded, load_sem.at[t]).wait()

        def step(i, carry):
            kappa = 1 - lax.div(i, 4)
            dz0, dz1 = lax.rem(lax.div(i, 2), 2), lax.rem(i, 2)
            kk = other(kappa)
            zz = flip_if(flip_if(z, kk, dz0), 1 - kk, dz1)
            weights = fac[zz]
            begin = pl.multiple_of(32 * STARTS[t] + kappa * 16 * size, 16)
            rows = left[pl.ds(begin, 16 * size), :]
            total = jnp.dot(rows, weights, preferred_element_type=jnp.float32)
            for j, (n, a) in enumerate(((3 * dz0, 0), (2 - dz0, dz0), (1 + dz0, dz0), (3 - 3 * dz0, 1))):
                slot[kappa, n, a, dz1, 0 : 4 * size] = total[j * 4 * size : (j + 1) * 4 * size]
            return carry

        lax.fori_loop(0, 4, step, 0)
        if t == 0:
            pl.semaphore_wait(barrier, len(greeted))
            for kappa, n in messages:
                index_copy(kappa, n).start()
        for kappa, n in messages:
            if kappa == 1:
                stage1(t, kappa, n).start()
        lax.fori_loop(4, 8, step, 0)
        for kappa, n in messages:
            if kappa == 0:
                stage1(t, kappa, n).start()
        for a in range(2):
            for rz in range(2):
                own[a, rz, 4 * STARTS[t] : 4 * (STARTS[t] + size), :] = (
                    slot[0, 0, a, rz, 0 : 4 * size, :].astype(jnp.bfloat16)
                )

    def stage1(t, kappa, n):
        return pltpu.make_async_remote_copy(
            src_ref=send[t % SLOTS].at[kappa, n, :, :, 0 : 4 * SIZES[t], :],
            dst_ref=recv[t].at[kappa * 4 + n - 1],
            send_sem=s1_ssem.at[t % SLOTS, kappa * 4 + n - 1],
            recv_sem=s1_rsem.at[t, kappa * 4 + n - 1],
            device_id=star_peer(kappa, n),
            device_id_type=MESH,
        )

    messages = [(1, 3), (1, 2), (1, 1), (0, 3), (0, 2), (0, 1), (1, 0)]

    def index_copy(kappa, n):
        return pltpu.make_async_remote_copy(
            src_ref=index_send,
            dst_ref=index_recv.at[kappa * 4 + n],
            send_sem=index_ssem.at[kappa * 4 + n - 1],
            recv_sem=index_rsem.at[kappa * 4 + n - 1],
            device_id=star_peer(kappa, n),
            device_id_type=MESH,
        )

    def own_block(a, rz):
        return flip_if(flip_if(z, star, a), rest, rz)

    def index_columns():
        for kappa, n in messages:
            index_copy(kappa, n).wait()
        index_recv[0] = index_send[...]

        def step(i, carry):
            zz = own_block(lax.div(i, 2), lax.rem(i, 2))
            rows = [index_recv[m, pl.ds(zz, 1), :] for m in range(8)]
            rows = jnp.concatenate(rows + [jnp.full((120, cap), -1, jnp.int32)], axis=0)
            columns[i] = rows.T.astype(jnp.int16)
            return carry

        lax.fori_loop(0, 4, step, 0)

    def assemble(t):
        size = SIZES[t]
        for kappa, n in messages:
            stage1(t, kappa, n).wait_recv()

        def step(i, carry):
            a, rz = lax.div(i, 2), lax.rem(i, 2)
            listed = columns[i]
            lanes = lax.broadcasted_iota(jnp.int32, (cap, block), 1).astype(jnp.int16)
            one, zero = jnp.bfloat16(1), jnp.bfloat16(0)
            for m in range(8):
                if m == 0:
                    piece = own[a, rz, 4 * STARTS[t] : 4 * (STARTS[t] + size), :]
                else:
                    piece = recv[t][m - 1, a, rz].astype(jnp.bfloat16)
                wide[0 : 4 * size, m * cap : (m + 1) * cap] = piece
                chosen = listed[:, m : m + 1] == lanes
                onehot[m * cap : (m + 1) * cap, :] = jnp.where(chosen, one, zero)
            total = jnp.dot(
                wide[0 : 4 * size, :], onehot[...], preferred_element_type=jnp.float32
            )
            dense[t][a, rz] = total.reshape(2, 2, size, block)
            return carry

        lax.fori_loop(0, 4, step, 0)

    def rows_of(t):
        return slice(STARTS[t], STARTS[t] + SIZES[t])

    def axis_of(t, stripe, stage):
        return (t + stripe + stage) % 3

    def part(t, stripe, stage, side):
        where = [slice(None)] * 3
        for before in range(stage):
            where[axis_of(t, stripe, before)] = 0
        where[axis_of(t, stripe, stage)] = side
        begin, width = STRIPES[stripe]
        return (slice(None), *where, slice(None), slice(begin, begin + width))

    def landing(stripe, stage):
        begin, width = STRIPES[stripe]
        return (*[slice(None)] * (4 - stage), slice(begin, begin + width))

    def halving(t, stripe, stage):
        return pltpu.make_async_remote_copy(
            src_ref=dense[t].at[part(t, stripe, stage, 1)],
            dst_ref=halves[stage][t].at[landing(stripe, stage)],
            send_sem=h_ssem.at[t, stage, stripe],
            recv_sem=h_rsem.at[t, stage, stripe],
            device_id=rest_peer(axis_of(t, stripe, stage)),
            device_id_type=MESH,
        )

    def crossing(t):
        return pltpu.make_async_remote_copy(
            src_ref=dense[t].at[1, 0, 0, 0],
            dst_ref=half3[t],
            send_sem=a_ssem.at[t],
            recv_sem=a_rsem.at[t],
            device_id=antipode,
            device_id_type=MESH,
        )

    def first(t):
        assemble(t)
        for stripe in range(3):
            halving(t, stripe, 0).start()

    def later(t, stage):
        for stripe in range(3):
            halving(t, stripe, stage - 1).wait_recv()
            where = part(t, stripe, stage - 1, 0)
            dense[t][where] = dense[t][where] + halves[stage - 1][t][landing(stripe, stage - 1)]
            if stage < 3:
                halving(t, stripe, stage).start()
        if stage == 3:
            crossing(t).start()

    def last(t):
        crossing(t).wait_recv()
        rows = rows_of(t)
        corrected[rows, :] = corrected[rows, :] - (dense[t][0, 0, 0, 0] + half3[t][...])

    def late_load(d):
        begin = pl.multiple_of((z + d) * block, block)
        return pltpu.make_async_copy(
            rows_factor.at[:, pl.ds(begin, block)], left.at[(d - 1) * block : d * block], late_sem.at[d]
        )

    inverse_load = pltpu.make_async_copy(inverse, left.at[3 * block : 4 * block], late_sem.at[0])

    def pending(station, d, t):
        rows = pl.ds(t * size, size)
        return pltpu.make_async_remote_copy(
            src_ref=pend_out.at[d - 1, rows, :],
            dst_ref=pend_in.at[station, rows, :],
            send_sem=p_ssem.at[d - 1, t],
            recv_sem=p_rsem.at[station, t],
            device_id=device(station + d, y, x, core),
            device_id_type=MESH,
        )

    def solve(station, t):
        rows = slice(t * size, (t + 1) * size)
        reduced = corrected[rows, :]
        for earlier in range(station):
            pending(earlier, station - earlier, t).wait_recv()
            reduced = reduced - pend_in[earlier, rows, :]
        solved = jnp.dot(
            reduced.astype(jnp.bfloat16), left[3], preferred_element_type=jnp.float32
        )
        out[rows, :] = solved
        for d in range(1, 4 - station):
            pend_out[d - 1, rows, :] = jnp.dot(
                solved.astype(jnp.bfloat16), left[d - 1], preferred_element_type=jnp.float32
            )
            pending(station, d, t).start()

    def solve_after(t):
        for station in range(4):
            chunks = [t - station] if t < CHUNKS - 1 else range(max(0, t - station), CHUNKS)
            if t - station >= 0 or t == CHUNKS - 1:
                @pl.when(z == station)
                def _(station=station, chunks=chunks):
                    for chunk in chunks:
                        solve(station, chunk)

    def pending(station, d, t):
        return pltpu.make_async_remote_copy(
            src_ref=half0[t].at[(0, d // 3, (d - 1) % 2)],
            dst_ref=pend_in.at[station, rows_of(t), :],
            send_sem=p_ssem.at[d - 1, t],
            recv_sem=p_rsem.at[station, t],
            device_id=device(station + d, y, x, core),
            device_id_type=MESH,
        )

    def spread(station, d, t, solved):
        half0[t][0, d // 3, (d - 1) % 2] = jnp.dot(
            solved.astype(jnp.bfloat16),
            left[(d - 1) * block : d * block, :],
            preferred_element_type=jnp.float32,
        )
        pending(station, d, t).start()

    def solve(station, t):
        rows = rows_of(t)
        reduced = corrected[rows, :]
        for earlier in range(station):
            pending(earlier, station - earlier, t).wait_recv()
            reduced = reduced - pend_in[earlier, rows, :]
        solved = jnp.dot(
            reduced.astype(jnp.bfloat16),
            left[3 * block : 4 * block, :],
            preferred_element_type=jnp.float32,
        )
        out[rows, :] = solved
        if station < 3:
            spread(station, 1, t, solved)
        for before in ([t - 1] if t else []) + ([t] if t == CHUNKS - 1 else []):
            for d in range(2, 4 - station):
                spread(station, d, before, out[rows_of(before), :])

    def solve_after(t):
        for station in range(4):
            lag = LAGS[station]
            chunks = [t - lag] if t < CHUNKS - 1 else list(range(max(0, t - lag), CHUNKS))
            if t - lag >= 0 or t == CHUNKS - 1:
                @pl.when(z == station)
                def _(station=station, chunks=chunks):
                    for chunk in chunks:
                        solve(station, chunk)

    def finish(t):
        last(t)
        solve_after(t)

    def products(t):
        if t + 1 < CHUNKS:
            load_rows(t + 1)
        if t >= SLOTS:
            for kappa, n in messages:
                stage1(t - SLOTS, kappa, n).wait_send()
        updates(t)
        if t == 1:
            base_copy.start()
        if t == CHUNKS - 1:
            for d in range(1, 4):
                @pl.when(z + d < 4)
                def _(d=d):
                    late_load(d).start()
            inverse_load.start()

    crossed = []
    for name, t in STEPS:
        if name == 0:
            products(t)
        elif name == 1:
            if t == 0:
                index_columns()
            first(t)
        elif name < 5:
            later(t, name - 1)
        else:
            if not crossed:
                for d in range(1, 4):
                    @pl.when(z + d < 4)
                    def _(d=d):
                        late_load(d).wait()
                inverse_load.wait()
                base_copy.wait()
            crossed.append(t)
            finish(t)

    for station in range(3):
        @pl.when(z == station)
        def _(station=station):
            for t in range(CHUNKS):
                for d in range(1, 4 - station):
                    pending(station, d, t).wait_send()
    for kappa, n in messages:
        for t in range(max(0, CHUNKS - SLOTS), CHUNKS):
            stage1(t, kappa, n).wait_send()
    for t in range(CHUNKS):
        for stripe in range(3):
            for stage in range(3):
                halving(t, stripe, stage).wait_send()
        crossing(t).wait_send()


def local(desc_rows, upd_factor, update_index, owner_map, sep_rhs, factor_rows, diag_inverse):
    tile, block = sep_rhs.shape
    cap = update_index.shape[1] // 4
    f32, bf16, i32 = jnp.float32, jnp.bfloat16, jnp.int32
    vmem = pl.BlockSpec(memory_space=pltpu.VMEM)
    hbm = pl.BlockSpec(memory_space=pl.ANY)
    dma = pltpu.SemaphoreType.DMA
    most = max(SIZES)
    chunked = [pltpu.VMEM((2, 4, 2, 2, 4 * most, cap), f32) for _ in range(SLOTS)]
    for lead in ((7, 2, 2, 4), (2, 2, 2, 2), (2, 2, 2), (2, 2), (2,), ()):
        for size in SIZES:
            if len(lead) == 4 and lead[0] == 7:
                chunked.append(pltpu.VMEM((7, 2, 2, 4 * size, cap), f32))
            else:
                chunked.append(pltpu.VMEM((*lead, size, block), f32))
    return pl.pallas_call(
        kernel,
        out_shape=jax.ShapeDtypeStruct((tile, block), f32),
        in_specs=[pl.BlockSpec(memory_space=pltpu.SMEM), vmem, hbm, hbm, hbm, hbm, hbm],
        out_specs=vmem,
        scratch_shapes=[
            pltpu.VMEM((32 * tile, block), bf16),
            pltpu.VMEM((4, block, cap), bf16),
            pltpu.VMEM((2, 2, 4 * tile, cap), bf16),
            pltpu.VMEM((8, cap), i32),
            pltpu.VMEM((8, 8, cap), i32),
            pltpu.VMEM((4, cap, 128), jnp.int16),
            pltpu.VMEM((8 * cap, block), bf16),
            pltpu.VMEM((4 * most, 8 * cap), bf16),
            pltpu.VMEM((tile, block), f32),
            pltpu.VMEM((3, tile, block), f32),
            dma((CHUNKS,)),
            dma((2,)),
            dma((4,)),
            dma((7,)),
            dma((7,)),
            dma((SLOTS, 7)),
            dma((CHUNKS, 7)),
            dma((CHUNKS, 3, 3)),
            dma((CHUNKS, 3, 3)),
            dma((CHUNKS,)),
            dma((CHUNKS,)),
            dma((3, CHUNKS)),
            dma((3, CHUNKS)),
            *chunked,
        ],
        compiler_params=pltpu.CompilerParams(
            collective_id=0, has_side_effects=True, vmem_limit_bytes=67_000_000
        ),
    )(owner_map, update_index, desc_rows, upd_factor, sep_rhs, factor_rows, diag_inverse)


def solution(mesh):
    placed = (
        P(("col", "rhs"), None, None),
        P(("col", "rhs"), None, None),
        P(("col", "rhs"), None),
        P(("col", "rhs"), None),
        P("rhs", "col"),
        P("col", None),
        P("col", None),
    )
    return jax.shard_map(
        local, mesh=mesh, in_specs=placed, out_specs=P("rhs", "col"), check_vma=False
    )
```

time: 157 us -> 124 us (0.79)
  Pallas kernels: 155 us -> 122 us
    pallas_call x1, Pallas kernels: 155 us -> 122 us  [local(): pl.pallas_call(kernel, out_shape=jax.ShapeDtypeStruct((tile, block), f32)...]
where the time goes in v2:
time: 124 us
  Pallas kernels  122 us (98%)
  local copies, waits for them, and re-layouts  1.89 us (2%)
    pallas_call x1, Pallas kernels, local(): pl.pallas_call(kernel, out_shape=jax.ShapeDtypeStruct((tile, block), f32)...  122 us

profile of v2, /device:TPU:96, one launch (start us, length us, event | category | flops | bytes accessed | tf_op | source)
XLA Modules:
  0.0 123.6 jit_solution(8654603128229413709)
XLA Ops:
  0.0 121.7 %shard_map.73 = f32[128,1024]{1,0:T(8,128)} custom-call(s32[1,4]{1,0:T(1,128)} %owner.1, s32[1,1024]{1,0:T(1,128)} %index.1, bf16[1,4096,1024]{2,1,0:T(8,128)(2,1)} %desc.1, bf16[1,1024,1024]{2,1,0:T(8,128)(2,1)} %factor.1, f32[128,1024]{1,0:T(8,128)} %sep.1, bf16[1024,4096]{1,0:T(8,128)(2,1)} %rows_factor.1, bf16[1024,1024]{1,0:T(8,128)(2,1)} %inverse.1), custom_call_target="tpu_custom_call" | custom-call | tf_op jit(solution)/shard_map/pallas_call | solution.py:456
  121.7 1.9 %copy.9 = f32[128,1024]{1,0:T(8,128)} copy(f32[128,1024]{1,0:T(8,128)} %shard_map.73) | data formatting | bytes 1048576

commit v3 on v2

--- a/solution.py
+++ b/solution.py
@@ -13,13 +13,15 @@
 CHUNKS = len(SIZES)
 SLOTS = 3
 STRIPES = ((0, 384), (384, 384), (768, 256))
+AXES = tuple(tuple(tuple((t + i + j) % 3 for j in range(3)) for i in range(3)) for t in range(3))
 STEPS = (
-    (0, 0), (0, 1), (1, 0), (0, 2), (1, 1), (0, 3), (2, 0), (1, 2),
-    (0, 4), (2, 1), (1, 3), (3, 0), (2, 2), (1, 4), (3, 1), (2, 3),
-    (4, 0), (3, 2), (2, 4), (5, 0), (4, 1), (3, 3), (4, 2), (3, 4),
-    (4, 3), (5, 1), (4, 4), (5, 2), (5, 3), (5, 4),
+    (0, 0), (0, 1), (1, 0), (0, 2), (2, 0), (0, 3), (3, 0), (1, 2),
+    (0, 4), (1, 1), (2, 2), (1, 3), (4, 0), (2, 1), (1, 4), (5, 0),
+    (3, 2), (3, 1), (2, 3), (4, 1), (2, 4), (3, 3), (3, 4), (4, 2),
+    (4, 3), (5, 1), (6, 0), (5, 2), (6, 1), (7, 0), (4, 4), (5, 3),
+    (6, 2), (7, 1), (8, 0), (5, 4), (6, 3), (7, 2), (8, 1), (6, 4),
+    (7, 3), (8, 2), (7, 4), (8, 3), (8, 4),
 )
-LAGS = (0, 1, 2, 3)
 
 
 def flip(place, bit):
@@ -32,10 +34,10 @@
     return place + wanted * (flip(place, bit) - place)
 
 
-def kernel(owner, index, desc, factor, sep, rows_factor, inverse, out,
-           left, fac, own, index_send, index_recv, columns, onehot, wide, corrected, pend_in,
+def kernel(owner, index, desc, factor, sep, rows_factor, inverse, out_hbm,
+           left, fac, own, index_send, index_recv, columns, onehot, wide, corrected, out, pend_in,
            load_sem, misc_sem, late_sem, index_ssem, index_rsem, s1_ssem, s1_rsem,
-           h_ssem, h_rsem, a_ssem, a_rsem, p_ssem, p_rsem, *chunked):
+           h_ssem, h_rsem, a_ssem, a_rsem, p_ssem, p_rsem, out_sem, *chunked):
     block = inverse.shape[0]
     cap = index.shape[1] // 4
     tile = sep.shape[0]
@@ -77,6 +79,9 @@
         )
 
     antipode = device(flip(z, star), flip(y, star), flip(x, star), core)
+
+    fac_copy = pltpu.make_async_copy(factor.at[0], fac_raw, misc_sem.at[0])
+    fac_copy.start()
 
     barrier = pltpu.get_barrier_semaphore()
     greeted = [device(z, y, x, 1 - core), antipode]
@@ -89,8 +94,6 @@
     for peer in greeted:
         pl.semaphore_signal(barrier, inc=1, device_id=peer, device_id_type=MESH)
 
-    fac_copy = pltpu.make_async_copy(factor.at[0], fac_raw, misc_sem.at[0])
-    fac_copy.start()
     def load_rows(t):
         size = SIZES[t]
 
@@ -158,6 +161,8 @@
         for kappa, n in messages:
             if kappa == 1:
                 stage1(t, kappa, n).start()
+        if t + 1 < CHUNKS:
+            load_rows(t + 1)
         lax.fori_loop(4, 8, step, 0)
         for kappa, n in messages:
             if kappa == 0:
@@ -237,7 +242,7 @@
         return slice(STARTS[t], STARTS[t] + SIZES[t])
 
     def axis_of(t, stripe, stage):
-        return (t + stripe + stage) % 3
+        return AXES[t % len(AXES)][stripe][stage]
 
     def part(t, stripe, stage, side):
         where = [slice(None)] * 3
@@ -300,42 +305,6 @@
     inverse_load = pltpu.make_async_copy(inverse, left.at[3 * block : 4 * block], late_sem.at[0])
 
     def pending(station, d, t):
-        rows = pl.ds(t * size, size)
-        return pltpu.make_async_remote_copy(
-            src_ref=pend_out.at[d - 1, rows, :],
-            dst_ref=pend_in.at[station, rows, :],
-            send_sem=p_ssem.at[d - 1, t],
-            recv_sem=p_rsem.at[station, t],
-            device_id=device(station + d, y, x, core),
-            device_id_type=MESH,
-        )
-
-    def solve(station, t):
-        rows = slice(t * size, (t + 1) * size)
-        reduced = corrected[rows, :]
-        for earlier in range(station):
-            pending(earlier, station - earlier, t).wait_recv()
-            reduced = reduced - pend_in[earlier, rows, :]
-        solved = jnp.dot(
-            reduced.astype(jnp.bfloat16), left[3], preferred_element_type=jnp.float32
-        )
-        out[rows, :] = solved
-        for d in range(1, 4 - station):
-            pend_out[d - 1, rows, :] = jnp.dot(
-                solved.astype(jnp.bfloat16), left[d - 1], preferred_element_type=jnp.float32
-            )
-            pending(station, d, t).start()
-
-    def solve_after(t):
-        for station in range(4):
-            chunks = [t - station] if t < CHUNKS - 1 else range(max(0, t - station), CHUNKS)
-            if t - station >= 0 or t == CHUNKS - 1:
-                @pl.when(z == station)
-                def _(station=station, chunks=chunks):
-                    for chunk in chunks:
-                        solve(station, chunk)
-
-    def pending(station, d, t):
         return pltpu.make_async_remote_copy(
             src_ref=half0[t].at[(0, d // 3, (d - 1) % 2)],
             dst_ref=pend_in.at[station, rows_of(t), :],
@@ -352,6 +321,10 @@
             preferred_element_type=jnp.float32,
         )
         pending(station, d, t).start()
+
+    def out_copy(t):
+        rows = rows_of(t)
+        return pltpu.make_async_copy(out.at[rows, :], out_hbm.at[rows, :], out_sem.at[t])
 
     def solve(station, t):
         rows = rows_of(t)
@@ -365,29 +338,23 @@
             preferred_element_type=jnp.float32,
         )
         out[rows, :] = solved
+        out_copy(t).start()
         if station < 3:
             spread(station, 1, t, solved)
         for before in ([t - 1] if t else []) + ([t] if t == CHUNKS - 1 else []):
             for d in range(2, 4 - station):
                 spread(station, d, before, out[rows_of(before), :])
 
-    def solve_after(t):
-        for station in range(4):
-            lag = LAGS[station]
-            chunks = [t - lag] if t < CHUNKS - 1 else list(range(max(0, t - lag), CHUNKS))
-            if t - lag >= 0 or t == CHUNKS - 1:
-                @pl.when(z == station)
-                def _(station=station, chunks=chunks):
-                    for chunk in chunks:
-                        solve(station, chunk)
+    def station_solve(station, t):
+        @pl.when(z == station)
+        def _():
+            solve(station, t)
 
     def finish(t):
         last(t)
-        solve_after(t)
+        station_solve(0, t)
 
     def products(t):
-        if t + 1 < CHUNKS:
-            load_rows(t + 1)
         if t >= SLOTS:
             for kappa, n in messages:
                 stage1(t - SLOTS, kappa, n).wait_send()
@@ -411,6 +378,8 @@
             first(t)
         elif name < 5:
             later(t, name - 1)
+        elif name > 5:
+            station_solve(name - 5, t)
         else:
             if not crossed:
                 for d in range(1, 4):
@@ -432,6 +401,7 @@
         for t in range(max(0, CHUNKS - SLOTS), CHUNKS):
             stage1(t, kappa, n).wait_send()
     for t in range(CHUNKS):
+        out_copy(t).wait()
         for stripe in range(3):
             for stage in range(3):
                 halving(t, stripe, stage).wait_send()
@@ -457,7 +427,7 @@
         kernel,
         out_shape=jax.ShapeDtypeStruct((tile, block), f32),
         in_specs=[pl.BlockSpec(memory_space=pltpu.SMEM), vmem, hbm, hbm, hbm, hbm, hbm],
-        out_specs=vmem,
+        out_specs=hbm,
         scratch_shapes=[
             pltpu.VMEM((32 * tile, block), bf16),
             pltpu.VMEM((4, block, cap), bf16),
@@ -467,6 +437,7 @@
             pltpu.VMEM((4, cap, 128), jnp.int16),
             pltpu.VMEM((8 * cap, block), bf16),
             pltpu.VMEM((4 * most, 8 * cap), bf16),
+            pltpu.VMEM((tile, block), f32),
             pltpu.VMEM((tile, block), f32),
             pltpu.VMEM((3, tile, block), f32),
             dma((CHUNKS,)),
@@ -482,10 +453,11 @@
             dma((CHUNKS,)),
             dma((3, CHUNKS)),
             dma((3, CHUNKS)),
+            dma((CHUNKS,)),
             *chunked,
         ],
         compiler_params=pltpu.CompilerParams(
-            collective_id=0, has_side_effects=True, vmem_limit_bytes=67_000_000
+            collective_id=0, has_side_effects=True, vmem_limit_bytes=65_000_000
         ),
     )(owner_map, update_index, desc_rows, upd_factor, sep_rhs, factor_rows, diag_inverse)
 

time: 124 us -> 124 us (level)
  no operation moved by 1% of the time
where the time goes in v3:
time: 124 us
  Pallas kernels  122 us (98%)
  local copies, waits for them, and re-layouts  1.89 us (2%)
    pallas_call x1, Pallas kernels, local(): pl.pallas_call(kernel, out_shape=jax.ShapeDtypeStruct((tile, block), f32)...  122 us

profile of v3, /device:TPU:96, one launch (start us, length us, event | category | flops | bytes accessed | tf_op | source)
XLA Modules:
  0.0 123.9 jit_solution(3146778889160275236)
XLA Ops:
  0.0 122.0 %shard_map.73 = f32[128,1024]{1,0:T(8,128)} custom-call(s32[1,4]{1,0:T(1,128)} %owner.1, s32[1,1024]{1,0:T(1,128)} %index.1, bf16[1,4096,1024]{2,1,0:T(8,128)(2,1)} %desc.1, bf16[1,1024,1024]{2,1,0:T(8,128)(2,1)} %factor.1, f32[128,1024]{1,0:T(8,128)} %sep.1, bf16[1024,4096]{1,0:T(8,128)(2,1)} %rows_factor.1, bf16[1024,1024]{1,0:T(8,128)(2,1)} %inverse.1), custom_call_target="tpu_custom_call" | custom-call | tf_op jit(solution)/shard_map/pallas_call | solution.py:426
  122.0 1.9 %copy.9 = f32[128,1024]{1,0:T(8,128)} copy(f32[128,1024]{1,0:T(8,128)} %shard_map.73) | data formatting | bytes 1048576
